TPU v7x, 128 devices: a whole 4x4x4 slice. The times are simulated.
128 devices in a mesh: wide: 16 (over y_lo, z, core), narrow: 8 (over x, y_hi).
Axes of the slice: x: 4, y: 4 (y_hi: 2, y_lo: 2; y = y_hi * 2 + y_lo), z: 4, core: 2. Of those that a mesh axis runs over, the one named last changes fastest.
Arguments:
- fields: float32 [5, 16, 64, 256], P(None, 'wide', 'narrow'), may hold values from -2.1 to 6.1, as said below
- prior_modes: bfloat16 [124, 5, 16, 16384], P(None, None, 'wide', 'narrow'), may hold values from -360 to 360, as said below
Outputs:
- flow_state: float32 [5, 16, 64, 256], P(None, 'wide', 'narrow')
- factor: float32 [128, 128], replicated
Inputs may be any that keep to these rules, and one draw needn't show every extreme that they name: `fields`: density and pressure lie in 0.6 to 1.4, each velocity component below 1.5 in magnitude. `prior_modes`: the columns are linearly independent.
All inputs are finite; a program needn't handle non-finite values.
Results may differ from a plain program's by a relative error of at most 0.0014.
Values may be sent and summed in bfloat16 or wider, within the bound.
No kernel may reach another device: no remote copies, remote signals or barrier semaphores. Data moves between devices by JAX's collectives and lax.ppermute only.
A program may use at most 64 MiB of HBM per device.

v0:
```python
import jax
import jax.numpy as jnp
from jax import lax
from jax.sharding import PartitionSpec as P

STEPS = 2
GAMMA = 1.4
TIME_STEP = 0.25
VISCOSITY = 0.15


def extended(block, sides, width):
    for axis, dim in sides:
        count = lax.axis_size(axis)
        forward = [(i, i + 1) for i in range(count - 1)]
        forward.append((count - 1, 0))
        backward = [(target, source) for source, target in forward]
        low = lax.ppermute(
            lax.slice_in_dim(block, block.shape[dim] - width, None, axis=dim), axis, forward
        )
        high = lax.ppermute(lax.slice_in_dim(block, 0, width, axis=dim), axis, backward)
        block = jnp.concatenate([low, block, high], axis=dim)
    return block


def flux_of(current, dim_index):
    density = current[0]
    momentum = current[1:4]
    energy = current[4]
    vel_d = momentum[dim_index] / density
    pressure = (GAMMA - 1.0) * (
        energy
        - 0.5
        * (momentum[0] * momentum[0] + momentum[1] * momentum[1] + momentum[2] * momentum[2])
        / density
    )
    components = [
        momentum[dim_index],
        momentum[0] * vel_d,
        momentum[1] * vel_d,
        momentum[2] * vel_d,
        (energy + pressure) * vel_d,
    ]
    components[1 + dim_index] = components[1 + dim_index] + pressure
    return jnp.stack(components)


def tendency(current):
    padded = extended(current.astype(jnp.bfloat16), (("wide", 1), ("narrow", 2)), 1).astype(
        current.dtype
    )
    flux_x = flux_of(padded[:, :, 1:-1], 0)
    flux_y = flux_of(padded[:, 1:-1, :], 1)
    flux_z = flux_of(current, 2)
    divergence = (
        flux_x[:, 2:]
        - flux_x[:, :-2]
        + (flux_y[:, :, 2:] - flux_y[:, :, :-2])
        + (jnp.roll(flux_z, -1, 3) - jnp.roll(flux_z, 1, 3))
    )
    laplace = (
        padded[:, 2:, 1:-1]
        + padded[:, :-2, 1:-1]
        + padded[:, 1:-1, 2:]
        + padded[:, 1:-1, :-2]
        + jnp.roll(current, -1, 3)
        + jnp.roll(current, 1, 3)
        - 6.0 * current
    )
    return -0.5 * divergence + VISCOSITY * laplace


def local(fields, prior_modes):
    wide_count = lax.axis_size("wide")
    narrow_count = lax.axis_size("narrow")
    cells_x, cells_y, cells_z = (fields.shape[1], fields.shape[2], fields.shape[3])
    inverse_cells = 1.0 / (cells_x * wide_count * cells_y * narrow_count * cells_z)
    flat_modes = prior_modes.reshape(prior_modes.shape[0], -1)
    contract = (((1,), (1,)), ((), ()))
    gram_modes = lax.dot_general(
        flat_modes, flat_modes, contract, preferred_element_type=jnp.float32
    )
    current = fields
    snapshots = []
    for step_index in range(STEPS):
        section_one = current + TIME_STEP * tendency(current)
        snapshots.append(section_one.astype(jnp.bfloat16))
        current = 0.5 * current + 0.5 * (section_one + TIME_STEP * tendency(section_one))
        snapshots.append(current.astype(jnp.bfloat16))
    arrived = lax.all_to_all(
        jnp.stack(snapshots), "narrow", split_axis=4, concat_axis=3, tiled=True
    )
    snap_rows = jnp.swapaxes(arrived, 3, 4).reshape(arrived.shape[0], -1)
    cross_gram = lax.dot_general(
        flat_modes, snap_rows, contract, preferred_element_type=jnp.float32
    )
    snap_gram = lax.dot_general(snap_rows, snap_rows, contract, preferred_element_type=jnp.float32)
    gram_local = jnp.concatenate(
        [
            jnp.concatenate([gram_modes, cross_gram], 1),
            jnp.concatenate([cross_gram.T, snap_gram], 1),
        ],
        0,
    )
    gram_local = gram_local * inverse_cells
    gram_whole = lax.psum(gram_local, ("wide", "narrow"))
    factor = jnp.linalg.cholesky(gram_whole).T
    return (current, factor)


def solution(mesh):
    placed = (P(None, "wide", "narrow", None), P(None, None, "wide", "narrow"))
    return jax.shard_map(
        local,
        mesh=mesh,
        in_specs=placed,
        out_specs=(P(None, "wide", "narrow", None), P()),
        check_vma=False,
    )
```

profile of v0, /device:TPU:1, one launch (start us, length us, event | category | flops | bytes accessed | tf_op | source)
XLA Modules:
  0.0 256.1 jit_solution(13830206497082720852)
XLA Ops:
  7.2 0.8 convert_element_type.30
  7.9 1.4 collective-permute-start.1
  9.3 1.6 collective-permute-start
  11.0 0.7 constant_dynamic-update-slice_fusion.14
  11.7 0.8 constant_dynamic-update-slice_fusion.13
  12.4 0.7 constant_dynamic-update-slice_fusion.12
  13.1 0.8 constant_dynamic-update-slice_fusion.11
  13.9 0.7 constant_dynamic-update-slice_fusion.10
  14.6 0.9 fusion.98
  15.7 5.2 %collective-permute-start.3 = (bf16[5,3,1,256]{3,1,2,0:T(4,128)(2,1)S(1)}, bf16[5,3,1,256]{3,1,2,0:T(4,128)(2,1)S(1)}, u32[]{:S(2)}, u32[]{:S(2)}) collective-permute-start(bf16[5,3,1,256]{3,1,2,0:T(4,128)(2,1)S(1)} %copy.427), channel_id=1, source_target_pairs={{1,0},{2,1},{3,2},{4,3},{5,4},{6,5},{7,6},{0,7},{9,8},{10,9},{11,1... | collective-permute-start | bytes 23048 | tf_op jit(solution)/shard_map/ppermute | solution.py:21
  20.8 0.8 fusion.99
  21.7 5.3 %collective-permute-done.2 = bf16[5,3,1,256]{3,1,2,0:T(4,128)(2,1)S(1)} collective-permute-done((bf16[5,3,1,256]{3,1,2,0:T(4,128)(2,1)S(1)}, bf16[5,3,1,256]{3,1,2,0:T(4,128)(2,1)S(1)}, u32[]{:S(2)}, u32[]{:S(2)}) %collective-permute-start.2) | collective-permute-done | bytes 7712 | tf_op jit(solution)/shard_map/ppermute | solution.py:18
  27.3 0.9 fusion.83
  28.2 4.9 %collective-permute-start.5 = (bf16[5,1,8,256]{3,2,0,1:T(8,128)(2,1)S(1)}, bf16[5,1,8,256]{3,2,0,1:T(8,128)(2,1)S(1)}, u32[]{:S(2)}, u32[]{:S(2)}) collective-permute-start(bf16[5,1,8,256]{3,2,0,1:T(8,128)(2,1)S(1)} %get-tuple-element.65), channel_id=1, source_target_pairs={{8,0},{16,8},{24,16},{32,24},{40,32},{48,40},{56,48},{64,56},{72,6... | collective-permute-start | bytes 61448 | tf_op jit(solution)/shard_map/ppermute | solution.py:21
  33.0 0.1 fusion.96
  33.2 0.1 fusion.94
  33.3 0.6 collective-permute-done.5
  33.9 1.0 collective-permute-done.4
  34.9 0.7 collective-permute-start.7
  35.6 2.3 collective-permute-start.6
  38.0 1.1 collective-permute-done.7
  39.1 2.6 %collective-permute-done.6 = bf16[5,3,1,256]{3,1,2,0:T(4,128)(2,1)S(1)} collective-permute-done((bf16[5,3,1,256]{3,1,2,0:T(4,128)(2,1)S(1)}, bf16[5,3,1,256]{3,1,2,0:T(4,128)(2,1)S(1)}, u32[]{:S(2)}, u32[]{:S(2)}) %collective-permute-start.6) | collective-permute-done | bytes 7712 | tf_op jit(solution)/shard_map/ppermute | solution.py:18
  42.1 0.1 broadcast_multiply_fusion
  42.2 0.1 fusion.92
  42.3 6.1 %collective-permute-start.9 = (bf16[5,1,8,256]{3,2,0,1:T(8,128)(2,1)S(1)}, bf16[5,1,8,256]{3,2,0,1:T(8,128)(2,1)S(1)}, u32[]{:S(2)}, u32[]{:S(2)}) collective-permute-start(bf16[5,1,8,256]{3,2,0,1:T(8,128)(2,1)S(1)} %fusion.78), channel_id=1, source_target_pairs={{8,0},{16,8},{24,16},{32,24},{40,32},{48,40},{56,48},{64,56},{72,6... | collective-permute-start | bytes 61448 | tf_op jit(solution)/shard_map/ppermute | solution.py:21
  48.5 0.1 fusion.90
  48.7 0.6 collective-permute-done.9
  49.3 0.3 collective-permute-done.8
  49.7 0.1 collective-permute-start.11
  49.8 2.9 %collective-permute-start.10 = (bf16[5,3,1,256]{3,1,2,0:T(4,128)(2,1)S(1)}, bf16[5,3,1,256]{3,1,2,0:T(4,128)(2,1)S(1)}, u32[]{:S(2)}, u32[]{:S(2)}) collective-permute-start(bf16[5,3,1,256]{3,1,2,0:T(4,128)(2,1)S(1)} %copy.394), channel_id=1, source_target_pairs={{0,1},{1,2},{2,3},{3,4},{4,5},{5,6},{6,7},{7,0},{8,9},{9,10},{10,1... | collective-permute-start | bytes 23048 | tf_op jit(solution)/shard_map/ppermute | solution.py:18
  52.8 1.0 collective-permute-done.11
  53.8 2.2 collective-permute-done.10
  56.3 0.1 fusion.80
  56.4 5.4 %collective-permute-start.13 = (bf16[5,1,8,256]{3,2,0,1:T(8,128)(2,1)S(1)}, bf16[5,1,8,256]{3,2,0,1:T(8,128)(2,1)S(1)}, u32[]{:S(2)}, u32[]{:S(2)}) collective-permute-start(bf16[5,1,8,256]{3,2,0,1:T(8,128)(2,1)S(1)} %get-tuple-element.31), channel_id=1, source_target_pairs={{8,0},{16,8},{24,16},{32,24},{40,32},{48,40},{56,48},{64,56},{72,6... | collective-permute-start | bytes 61448 | tf_op jit(solution)/shard_map/ppermute | solution.py:21
  62.0 0.1 fusion.86
  62.2 0.6 collective-permute-done.13
  62.7 0.3 collective-permute-done.12
  63.1 0.1 collective-permute-start.15
  63.2 2.9 %collective-permute-start.14 = (bf16[5,3,1,256]{3,1,2,0:T(4,128)(2,1)S(1)}, bf16[5,3,1,256]{3,1,2,0:T(4,128)(2,1)S(1)}, u32[]{:S(2)}, u32[]{:S(2)}) collective-permute-start(bf16[5,3,1,256]{3,1,2,0:T(4,128)(2,1)S(1)} %copy.405), channel_id=1, source_target_pairs={{0,1},{1,2},{2,3},{3,4},{4,5},{5,6},{6,7},{7,0},{8,9},{9,10},{10,1... | collective-permute-start | bytes 23048 | tf_op jit(solution)/shard_map/ppermute | solution.py:18
  66.2 1.0 collective-permute-done.15
  67.2 2.2 collective-permute-done.14
  69.7 0.7 convert_bitcast_fusion
  70.5 0.7 copy.416
  71.2 2.1 reshape.630
  73.3 3.4 %all-to-all-start = ((bf16[8,2,2560]{2,1,0:T(2,128)(2,1)}), bf16[8,2,2560]{2,1,0:T(2,128)(2,1)S(1)}, u32[]{:S(2)}, u32[]{:S(2)}) async-start(bf16[8,2,2560]{2,1,0:T(2,128)(2,1)} %reshape.630), calls=%async_computation | async-start | bytes 163840 | tf_op jit(solution)/shard_map/all_to_all | solution.py:90
  76.6 0.2 all-reduce.2.cloned.1.call-start
  76.9 3.4 %fusion.2 = f32[124,124]{0,1:T(8,128)S(1)} fusion(bf16[124,5,1,2048]{3,0,2,1:T(8,128)(2,1)} %param.3), kind=kOutput, calls=%fused_computation.2 | convolution fusion | flops 314900480 | bytes 2601024 | tf_op jit(solution)/shard_map/dot_general | solution.py:80
  80.2 3.3 %copy.420 = bf16[124,5,1,2048]{0,3,1,2:T(8,128)(2,1)S(1)} copy(bf16[124,5,1,2048]{3,0,2,1:T(8,128)(2,1)} %param.3) | data formatting | bytes 5079040 | tf_op args[1]
  83.6 2.6 %reshape.631 = bf16[256,5,1,4,8]{4,3,2,1,0:T(4,128)(2,1)} reshape(bf16[8,2,2560]{2,1,0:T(2,128)(2,1)S(1)} %all-to-all-done) | data formatting | bytes 163840
  86.2 1.8 copy.417
  88.0 0.2 copy.418
  88.2 0.3 convolution_bitcast_fusion
  88.5 0.2 reshape.625
  88.7 0.4 fusion.102
  89.1 0.1 pad_maximum_fusion.31
  89.2 0.1 copy.421
  89.3 0.7 maximum_multiply_fusion
  90.1 143.6 %all-reduce.2.cloned.1.call-done = f32[128,128]{0,1:T(8,128)} async-done(((f32[128,128]{0,1:T(8,128)}), f32[128,128]{0,1:T(8,128)}) %all-reduce.2.cloned.1.call-update) | async-done | bytes 65552 | tf_op jit(solution)/shard_map/psum | solution.py:106
  233.7 0.9 copy.422
  234.6 0.9 fusion.6
  235.5 11.7 %cholesky.18 = f32[128,128]{1,0:T(8,128)S(1)} custom-call(f32[128,128]{1,0:T(8,128)S(1)} %fusion.6), custom_call_target="Cholesky" | custom-call | tf_op jit(solution)/shard_map/jit(cholesky)/cholesky | solution.py:107
  247.2 0.6 compare_reduce_fusion
  247.9 0.7 select_bitcast_fusion
  248.5 0.7 copy.424
  (103 shorter events, 1.9 us)
Async XLA Ops:
  7.9 7.6 %collective-permute-start.1 = (bf16[5,1,8,256]{3,2,1,0:T(8,128)(2,1)S(1)}, bf16[5,1,8,256]{3,2,1,0:T(8,128)(2,1)S(1)}, u32[]{:S(2)}, u32[]{:S(2)}) collective-permute-start(bf16[5,1,8,256]{3,2,1,0:T(8,128)(2,1)S(1)} %convert_element_type.30), channel_id=1, source_target_pairs={{8,0},{16,8},{24,16},{32,24},{40,32},{48,40},{56,48},{64,56},{72,6... | collective-permute-start | bytes 61448 | tf_op jit(solution)/shard_map/ppermute | solution.py:21
  9.3 6.3 %collective-permute-start = (bf16[5,1,8,256]{3,2,1,0:T(8,128)(2,1)S(1)}, bf16[5,1,8,256]{3,2,1,0:T(8,128)(2,1)S(1)}, u32[]{:S(2)}, u32[]{:S(2)}) collective-permute-start(bf16[5,1,8,256]{3,2,1,0:T(8,128)(2,1)S(1)} %convert_element_type.30), channel_id=1, source_target_pairs={{0,8},{8,16},{16,24},{24,32},{32,40},{40,48},{48,56},{56,64},{64,7... | collective-permute-start | bytes 61448 | tf_op jit(solution)/shard_map/ppermute | solution.py:18
  11.7 30.4 %copy-start = (f32[5,1,8,256]{3,2,1,0:T(8,128)S(1)}, f32[5,1,8,256]{3,2,1,0:T(8,128)}, u32[]{:S(2)}) copy-start(f32[5,1,8,256]{3,2,1,0:T(8,128)} %param.2) | copy-start | bytes 122884
  15.7 6.0 %collective-permute-start.3 = (bf16[5,3,1,256]{3,1,2,0:T(4,128)(2,1)S(1)}, bf16[5,3,1,256]{3,1,2,0:T(4,128)(2,1)S(1)}, u32[]{:S(2)}, u32[]{:S(2)}) collective-permute-start(bf16[5,3,1,256]{3,1,2,0:T(4,128)(2,1)S(1)} %copy.427), channel_id=1, source_target_pairs={{1,0},{2,1},{3,2},{4,3},{5,4},{6,5},{7,6},{0,7},{9,8},{10,9},{11,1... | collective-permute-start | bytes 23048 | tf_op jit(solution)/shard_map/ppermute | solution.py:21
  20.8 6.1 %collective-permute-start.2 = (bf16[5,3,1,256]{3,1,2,0:T(4,128)(2,1)S(1)}, bf16[5,3,1,256]{3,1,2,0:T(4,128)(2,1)S(1)}, u32[]{:S(2)}, u32[]{:S(2)}) collective-permute-start(bf16[5,3,1,256]{3,1,2,0:T(4,128)(2,1)S(1)} %copy.426), channel_id=1, source_target_pairs={{0,1},{1,2},{2,3},{3,4},{4,5},{5,6},{6,7},{7,0},{8,9},{9,10},{10,1... | collective-permute-start | bytes 23048 | tf_op jit(solution)/shard_map/ppermute | solution.py:18
  28.2 5.7 %collective-permute-start.5 = (bf16[5,1,8,256]{3,2,0,1:T(8,128)(2,1)S(1)}, bf16[5,1,8,256]{3,2,0,1:T(8,128)(2,1)S(1)}, u32[]{:S(2)}, u32[]{:S(2)}) collective-permute-start(bf16[5,1,8,256]{3,2,0,1:T(8,128)(2,1)S(1)} %get-tuple-element.65), channel_id=1, source_target_pairs={{8,0},{16,8},{24,16},{32,24},{40,32},{48,40},{56,48},{64,56},{72,6... | collective-permute-start | bytes 61448 | tf_op jit(solution)/shard_map/ppermute | solution.py:21
  33.0 1.8 collective-permute-start.4
  34.9 4.2 %collective-permute-start.7 = (bf16[5,3,1,256]{3,1,2,0:T(4,128)(2,1)S(1)}, bf16[5,3,1,256]{3,1,2,0:T(4,128)(2,1)S(1)}, u32[]{:S(2)}, u32[]{:S(2)}) collective-permute-start(bf16[5,3,1,256]{3,1,2,0:T(4,128)(2,1)S(1)} %copy.383), channel_id=1, source_target_pairs={{1,0},{2,1},{3,2},{4,3},{5,4},{6,5},{7,6},{0,7},{9,8},{10,9},{11,1... | collective-permute-start | bytes 23048 | tf_op jit(solution)/shard_map/ppermute | solution.py:21
  35.6 6.1 %collective-permute-start.6 = (bf16[5,3,1,256]{3,1,2,0:T(4,128)(2,1)S(1)}, bf16[5,3,1,256]{3,1,2,0:T(4,128)(2,1)S(1)}, u32[]{:S(2)}, u32[]{:S(2)}) collective-permute-start(bf16[5,3,1,256]{3,1,2,0:T(4,128)(2,1)S(1)} %copy.382), channel_id=1, source_target_pairs={{0,1},{1,2},{2,3},{3,4},{4,5},{5,6},{6,7},{7,0},{8,9},{9,10},{10,1... | collective-permute-start | bytes 23048 | tf_op jit(solution)/shard_map/ppermute | solution.py:18
  42.3 7.0 %collective-permute-start.9 = (bf16[5,1,8,256]{3,2,0,1:T(8,128)(2,1)S(1)}, bf16[5,1,8,256]{3,2,0,1:T(8,128)(2,1)S(1)}, u32[]{:S(2)}, u32[]{:S(2)}) collective-permute-start(bf16[5,1,8,256]{3,2,0,1:T(8,128)(2,1)S(1)} %fusion.78), channel_id=1, source_target_pairs={{8,0},{16,8},{24,16},{32,24},{40,32},{48,40},{56,48},{64,56},{72,6... | collective-permute-start | bytes 61448 | tf_op jit(solution)/shard_map/ppermute | solution.py:21
  48.5 1.2 collective-permute-start.8
  49.7 4.1 %collective-permute-start.11 = (bf16[5,3,1,256]{3,1,2,0:T(4,128)(2,1)S(1)}, bf16[5,3,1,256]{3,1,2,0:T(4,128)(2,1)S(1)}, u32[]{:S(2)}, u32[]{:S(2)}) collective-permute-start(bf16[5,3,1,256]{3,1,2,0:T(4,128)(2,1)S(1)} %copy.395), channel_id=1, source_target_pairs={{1,0},{2,1},{3,2},{4,3},{5,4},{6,5},{7,6},{0,7},{9,8},{10,9},{11,1... | collective-permute-start | bytes 23048 | tf_op jit(solution)/shard_map/ppermute | solution.py:21
  49.8 6.2 %collective-permute-start.10 = (bf16[5,3,1,256]{3,1,2,0:T(4,128)(2,1)S(1)}, bf16[5,3,1,256]{3,1,2,0:T(4,128)(2,1)S(1)}, u32[]{:S(2)}, u32[]{:S(2)}) collective-permute-start(bf16[5,3,1,256]{3,1,2,0:T(4,128)(2,1)S(1)} %copy.394), channel_id=1, source_target_pairs={{0,1},{1,2},{2,3},{3,4},{4,5},{5,6},{6,7},{7,0},{8,9},{9,10},{10,1... | collective-permute-start | bytes 23048 | tf_op jit(solution)/shard_map/ppermute | solution.py:18
  56.4 6.3 %collective-permute-start.13 = (bf16[5,1,8,256]{3,2,0,1:T(8,128)(2,1)S(1)}, bf16[5,1,8,256]{3,2,0,1:T(8,128)(2,1)S(1)}, u32[]{:S(2)}, u32[]{:S(2)}) collective-permute-start(bf16[5,1,8,256]{3,2,0,1:T(8,128)(2,1)S(1)} %get-tuple-element.31), channel_id=1, source_target_pairs={{8,0},{16,8},{24,16},{32,24},{40,32},{48,40},{56,48},{64,56},{72,6... | collective-permute-start | bytes 61448 | tf_op jit(solution)/shard_map/ppermute | solution.py:21
  61.9 1.2 collective-permute-start.12
  63.1 4.1 %collective-permute-start.15 = (bf16[5,3,1,256]{3,1,2,0:T(4,128)(2,1)S(1)}, bf16[5,3,1,256]{3,1,2,0:T(4,128)(2,1)S(1)}, u32[]{:S(2)}, u32[]{:S(2)}) collective-permute-start(bf16[5,3,1,256]{3,1,2,0:T(4,128)(2,1)S(1)} %copy.406), channel_id=1, source_target_pairs={{1,0},{2,1},{3,2},{4,3},{5,4},{6,5},{7,6},{0,7},{9,8},{10,9},{11,1... | collective-permute-start | bytes 23048 | tf_op jit(solution)/shard_map/ppermute | solution.py:21
  63.2 6.2 %collective-permute-start.14 = (bf16[5,3,1,256]{3,1,2,0:T(4,128)(2,1)S(1)}, bf16[5,3,1,256]{3,1,2,0:T(4,128)(2,1)S(1)}, u32[]{:S(2)}, u32[]{:S(2)}) collective-permute-start(bf16[5,3,1,256]{3,1,2,0:T(4,128)(2,1)S(1)} %copy.405), channel_id=1, source_target_pairs={{0,1},{1,2},{2,3},{3,4},{4,5},{5,6},{6,7},{7,0},{8,9},{9,10},{10,1... | collective-permute-start | bytes 23048 | tf_op jit(solution)/shard_map/ppermute | solution.py:18
  73.3 10.3 %all-to-all-start = ((bf16[8,2,2560]{2,1,0:T(2,128)(2,1)}), bf16[8,2,2560]{2,1,0:T(2,128)(2,1)S(1)}, u32[]{:S(2)}, u32[]{:S(2)}) async-start(bf16[8,2,2560]{2,1,0:T(2,128)(2,1)} %reshape.630), calls=%async_computation | async-start | bytes 163840 | tf_op jit(solution)/shard_map/all_to_all | solution.py:90
  76.6 157.1 %all-reduce.2.cloned.1.call-start = ((), (), s32[]{:S(2)}) async-start(), calls=%async_computation.1 | async-start | bytes 131072 | tf_op jit(solution)/shard_map/psum | solution.py:106
Sparse Core Ops, SparseCore 0:
  90.2 143.4 all-reduce.1
where the time goes:
time: 257 us; the launch traced here: 256 us
  waiting for transfers between devices  162 us (63%)
  starting transfers between devices  37.3 us (15%)
  other arithmetic  21.4 us (8%)
  local copies, waits for them, and re-layouts  16.3 us (6%)
  between operations  14.7 us (6%)
  matrix products  4.08 us (2%)
    psum x1, waiting for transfers between devices, local(): gram_whole = lax.psum(gram_local, ('wide', 'narrow'))  144 us
    ppermute x8, starting transfers between devices, extended(): lax.ppermute(lax.slice_in_dim(block, 0, width, axis=dim), axis, backward)  23.8 us
    ppermute x8, waiting for transfers between devices, extended(): lax.ppermute(lax.slice_in_dim(block, block.shape[dim] - width, None, axis...  13.9 us
    another operation x3, other arithmetic, local(): factor = jnp.linalg.cholesky(gram_whole).T  12.4 us
    ppermute x8, starting transfers between devices, extended(): lax.ppermute(lax.slice_in_dim(block, block.shape[dim] - width, None, axis...  9.89 us
    unnamed x16, local copies, waits for them, and re-layouts  9.47 us
  transfers between devices with their start and end apart: 18, of which 14 were waited for; matrix products, arithmetic and copies ran while one was open for 5% of the time, Pallas kernels for 0%

commit v1 on v0

--- a/solution.py
+++ b/solution.py
@@ -103,7 +103,7 @@
         0,
     )
     gram_local = gram_local * inverse_cells
-    gram_whole = lax.psum(gram_local, ("wide", "narrow"))
+    gram_whole = lax.psum(lax.psum(gram_local, "wide"), "narrow")
     factor = jnp.linalg.cholesky(gram_whole).T
     return (current, factor)
 

time: 257 us -> 312 us (1.21); the launches traced: 256 us -> 306 us
  waiting for transfers between devices: 162 us -> 213 us
    psum x1 -> x2, waiting for transfers between devices: 144 us -> 194 us  [local(): gram_whole = lax.psum(lax.psum(gram_local, 'wide'), 'narrow')]
  transfers between devices with their start and end apart: 18 -> 19, of which waited for: 14 -> 15; matrix products, arithmetic and copies ran while one was open for 5% -> 4% of each run, Pallas kernels for 0% -> 0%
where the time goes in v1:
time: 312 us; the launch traced here: 306 us
  waiting for transfers between devices  213 us (68%)
  starting transfers between devices  37.3 us (12%)
  other arithmetic  21.4 us (7%)
  local copies, waits for them, and re-layouts  16.3 us (5%)
  between operations  14.7 us (5%)
  matrix products  4.08 us (1%)
    psum x2, waiting for transfers between devices, local(): gram_whole = lax.psum(lax.psum(gram_local, 'wide'), 'narrow')  194 us
    ppermute x8, starting transfers between devices, extended(): lax.ppermute(lax.slice_in_dim(block, 0, width, axis=dim), axis, backward)  23.8 us
    ppermute x8, waiting for transfers between devices, extended(): lax.ppermute(lax.slice_in_dim(block, block.shape[dim] - width, None, axis...  13.9 us
    another operation x3, other arithmetic, local(): factor = jnp.linalg.cholesky(gram_whole).T  12.4 us
    ppermute x8, starting transfers between devices, extended(): lax.ppermute(lax.slice_in_dim(block, block.shape[dim] - width, None, axis...  9.89 us
    unnamed x16, local copies, waits for them, and re-layouts  9.47 us
  transfers between devices with their start and end apart: 19, of which 15 were waited for; matrix products, arithmetic and copies ran while one was open for 4% of the time, Pallas kernels for 0%

profile of v1, /device:TPU:1, one launch (start us, length us, event | category | flops | bytes accessed | tf_op | source)
XLA Modules:
  0.0 306.3 jit_solution(13559636637448301448)
XLA Ops:
  7.2 0.8 convert_element_type.30
  7.9 1.4 collective-permute-start.1
  9.3 1.6 collective-permute-start
  11.0 0.7 constant_dynamic-update-slice_fusion.14
  11.7 0.8 constant_dynamic-update-slice_fusion.13
  12.4 0.7 constant_dynamic-update-slice_fusion.12
  13.1 0.8 constant_dynamic-update-slice_fusion.11
  13.9 0.7 constant_dynamic-update-slice_fusion.10
  14.6 0.9 fusion.98
  15.7 5.2 %collective-permute-start.3 = (bf16[5,3,1,256]{3,1,2,0:T(4,128)(2,1)S(1)}, bf16[5,3,1,256]{3,1,2,0:T(4,128)(2,1)S(1)}, u32[]{:S(2)}, u32[]{:S(2)}) collective-permute-start(bf16[5,3,1,256]{3,1,2,0:T(4,128)(2,1)S(1)} %copy.427), channel_id=1, source_target_pairs={{1,0},{2,1},{3,2},{4,3},{5,4},{6,5},{7,6},{0,7},{9,8},{10,9},{11,1... | collective-permute-start | bytes 23048 | tf_op jit(solution)/shard_map/ppermute | solution.py:21
  20.8 0.8 fusion.99
  21.7 5.3 %collective-permute-done.2 = bf16[5,3,1,256]{3,1,2,0:T(4,128)(2,1)S(1)} collective-permute-done((bf16[5,3,1,256]{3,1,2,0:T(4,128)(2,1)S(1)}, bf16[5,3,1,256]{3,1,2,0:T(4,128)(2,1)S(1)}, u32[]{:S(2)}, u32[]{:S(2)}) %collective-permute-start.2) | collective-permute-done | bytes 7712 | tf_op jit(solution)/shard_map/ppermute | solution.py:18
  27.3 0.9 fusion.83
  28.2 4.9 %collective-permute-start.5 = (bf16[5,1,8,256]{3,2,0,1:T(8,128)(2,1)S(1)}, bf16[5,1,8,256]{3,2,0,1:T(8,128)(2,1)S(1)}, u32[]{:S(2)}, u32[]{:S(2)}) collective-permute-start(bf16[5,1,8,256]{3,2,0,1:T(8,128)(2,1)S(1)} %get-tuple-element.65), channel_id=1, source_target_pairs={{8,0},{16,8},{24,16},{32,24},{40,32},{48,40},{56,48},{64,56},{72,6... | collective-permute-start | bytes 61448 | tf_op jit(solution)/shard_map/ppermute | solution.py:21
  33.2 0.1 fusion.94
  33.3 0.6 collective-permute-done.5
  33.9 1.0 collective-permute-done.4
  34.9 0.7 collective-permute-start.7
  35.6 2.3 collective-permute-start.6
  38.0 1.1 collective-permute-done.7
  39.1 2.6 collective-permute-done.6
  42.1 0.1 broadcast_multiply_fusion
  42.2 0.1 fusion.92
  42.3 6.1 %collective-permute-start.9 = (bf16[5,1,8,256]{3,2,0,1:T(8,128)(2,1)S(1)}, bf16[5,1,8,256]{3,2,0,1:T(8,128)(2,1)S(1)}, u32[]{:S(2)}, u32[]{:S(2)}) collective-permute-start(bf16[5,1,8,256]{3,2,0,1:T(8,128)(2,1)S(1)} %fusion.78), channel_id=1, source_target_pairs={{8,0},{16,8},{24,16},{32,24},{40,32},{48,40},{56,48},{64,56},{72,6... | collective-permute-start | bytes 61448 | tf_op jit(solution)/shard_map/ppermute | solution.py:21
  48.5 0.1 fusion.90
  48.7 0.6 collective-permute-done.9
  49.3 0.3 collective-permute-done.8
  49.7 0.1 collective-permute-start.11
  49.8 2.9 collective-permute-start.10
  52.8 1.0 collective-permute-done.11
  53.8 2.2 collective-permute-done.10
  56.3 0.1 fusion.80
  56.4 5.4 %collective-permute-start.13 = (bf16[5,1,8,256]{3,2,0,1:T(8,128)(2,1)S(1)}, bf16[5,1,8,256]{3,2,0,1:T(8,128)(2,1)S(1)}, u32[]{:S(2)}, u32[]{:S(2)}) collective-permute-start(bf16[5,1,8,256]{3,2,0,1:T(8,128)(2,1)S(1)} %get-tuple-element.31), channel_id=1, source_target_pairs={{8,0},{16,8},{24,16},{32,24},{40,32},{48,40},{56,48},{64,56},{72,6... | collective-permute-start | bytes 61448 | tf_op jit(solution)/shard_map/ppermute | solution.py:21
  62.0 0.1 fusion.86
  62.2 0.6 collective-permute-done.13
  62.7 0.3 collective-permute-done.12
  63.1 0.1 collective-permute-start.15
  63.2 2.9 collective-permute-start.14
  66.2 1.0 collective-permute-done.15
  67.2 2.2 collective-permute-done.14
  69.7 0.7 convert_bitcast_fusion
  70.5 0.7 copy.416
  71.2 2.1 reshape.630
  73.3 3.4 %all-to-all-start = ((bf16[8,2,2560]{2,1,0:T(2,128)(2,1)}), bf16[8,2,2560]{2,1,0:T(2,128)(2,1)S(1)}, u32[]{:S(2)}, u32[]{:S(2)}) async-start(bf16[8,2,2560]{2,1,0:T(2,128)(2,1)} %reshape.630), calls=%async_computation | async-start | bytes 163840 | tf_op jit(solution)/shard_map/all_to_all | solution.py:90
  76.6 0.2 all-reduce.3.cloned.1.call-start
  76.9 3.4 %fusion.2 = f32[124,124]{0,1:T(8,128)S(1)} fusion(bf16[124,5,1,2048]{3,0,2,1:T(8,128)(2,1)} %param.3), kind=kOutput, calls=%fused_computation.2 | convolution fusion | flops 314900480 | bytes 2601024 | tf_op jit(solution)/shard_map/dot_general | solution.py:80
  80.2 3.3 %copy.420 = bf16[124,5,1,2048]{0,3,1,2:T(8,128)(2,1)S(1)} copy(bf16[124,5,1,2048]{3,0,2,1:T(8,128)(2,1)} %param.3) | data formatting | bytes 5079040 | tf_op args[1]
  83.6 2.6 reshape.631
  86.2 1.8 copy.417
  88.0 0.2 copy.418
  88.2 0.3 convolution_bitcast_fusion
  88.5 0.2 reshape.625
  88.7 0.4 fusion.102
  89.1 0.1 pad_maximum_fusion.31
  89.2 0.1 copy.421
  89.3 0.7 maximum_multiply_fusion
  90.1 109.8 %all-reduce.3.cloned.1.call-done = f32[128,128]{0,1:T(8,128)} async-done(((f32[128,128]{0,1:T(8,128)}), f32[128,128]{0,1:T(8,128)}) %all-reduce.3.cloned.1.call-update) | async-done | bytes 65552 | tf_op jit(solution)/shard_map/psum | solution.py:106
  199.9 84.0 %all-reduce.5.cloned.1.call-done = f32[128,128]{0,1:T(8,128)} async-done(((f32[128,128]{0,1:T(8,128)}), f32[128,128]{0,1:T(8,128)}) %all-reduce.5.cloned.1.call-update) | async-done | bytes 65552 | tf_op jit(solution)/shard_map/psum | solution.py:106
  283.9 0.9 copy.422
  284.8 0.9 fusion.6
  285.7 11.7 %cholesky.18 = f32[128,128]{1,0:T(8,128)S(1)} custom-call(f32[128,128]{1,0:T(8,128)S(1)} %fusion.6), custom_call_target="Cholesky" | custom-call | tf_op jit(solution)/shard_map/jit(cholesky)/cholesky | solution.py:107
  297.4 0.6 compare_reduce_fusion
  298.1 0.7 select_bitcast_fusion
  298.7 0.7 copy.424
  (106 shorter events, 2.0 us)
Async XLA Ops:
  7.9 7.6 %collective-permute-start.1 = (bf16[5,1,8,256]{3,2,1,0:T(8,128)(2,1)S(1)}, bf16[5,1,8,256]{3,2,1,0:T(8,128)(2,1)S(1)}, u32[]{:S(2)}, u32[]{:S(2)}) collective-permute-start(bf16[5,1,8,256]{3,2,1,0:T(8,128)(2,1)S(1)} %convert_element_type.30), channel_id=1, source_target_pairs={{8,0},{16,8},{24,16},{32,24},{40,32},{48,40},{56,48},{64,56},{72,6... | collective-permute-start | bytes 61448 | tf_op jit(solution)/shard_map/ppermute | solution.py:21
  9.3 6.3 %collective-permute-start = (bf16[5,1,8,256]{3,2,1,0:T(8,128)(2,1)S(1)}, bf16[5,1,8,256]{3,2,1,0:T(8,128)(2,1)S(1)}, u32[]{:S(2)}, u32[]{:S(2)}) collective-permute-start(bf16[5,1,8,256]{3,2,1,0:T(8,128)(2,1)S(1)} %convert_element_type.30), channel_id=1, source_target_pairs={{0,8},{8,16},{16,24},{24,32},{32,40},{40,48},{48,56},{56,64},{64,7... | collective-permute-start | bytes 61448 | tf_op jit(solution)/shard_map/ppermute | solution.py:18
  11.7 30.4 %copy-start = (f32[5,1,8,256]{3,2,1,0:T(8,128)S(1)}, f32[5,1,8,256]{3,2,1,0:T(8,128)}, u32[]{:S(2)}) copy-start(f32[5,1,8,256]{3,2,1,0:T(8,128)} %param.2) | copy-start | bytes 122884
  15.7 6.0 %collective-permute-start.3 = (bf16[5,3,1,256]{3,1,2,0:T(4,128)(2,1)S(1)}, bf16[5,3,1,256]{3,1,2,0:T(4,128)(2,1)S(1)}, u32[]{:S(2)}, u32[]{:S(2)}) collective-permute-start(bf16[5,3,1,256]{3,1,2,0:T(4,128)(2,1)S(1)} %copy.427), channel_id=1, source_target_pairs={{1,0},{2,1},{3,2},{4,3},{5,4},{6,5},{7,6},{0,7},{9,8},{10,9},{11,1... | collective-permute-start | bytes 23048 | tf_op jit(solution)/shard_map/ppermute | solution.py:21
  20.8 6.1 %collective-permute-start.2 = (bf16[5,3,1,256]{3,1,2,0:T(4,128)(2,1)S(1)}, bf16[5,3,1,256]{3,1,2,0:T(4,128)(2,1)S(1)}, u32[]{:S(2)}, u32[]{:S(2)}) collective-permute-start(bf16[5,3,1,256]{3,1,2,0:T(4,128)(2,1)S(1)} %copy.426), channel_id=1, source_target_pairs={{0,1},{1,2},{2,3},{3,4},{4,5},{5,6},{6,7},{7,0},{8,9},{9,10},{10,1... | collective-permute-start | bytes 23048 | tf_op jit(solution)/shard_map/ppermute | solution.py:18
  28.2 5.7 %collective-permute-start.5 = (bf16[5,1,8,256]{3,2,0,1:T(8,128)(2,1)S(1)}, bf16[5,1,8,256]{3,2,0,1:T(8,128)(2,1)S(1)}, u32[]{:S(2)}, u32[]{:S(2)}) collective-permute-start(bf16[5,1,8,256]{3,2,0,1:T(8,128)(2,1)S(1)} %get-tuple-element.65), channel_id=1, source_target_pairs={{8,0},{16,8},{24,16},{32,24},{40,32},{48,40},{56,48},{64,56},{72,6... | collective-permute-start | bytes 61448 | tf_op jit(solution)/shard_map/ppermute | solution.py:21
  33.0 1.8 collective-permute-start.4
  34.9 4.2 %collective-permute-start.7 = (bf16[5,3,1,256]{3,1,2,0:T(4,128)(2,1)S(1)}, bf16[5,3,1,256]{3,1,2,0:T(4,128)(2,1)S(1)}, u32[]{:S(2)}, u32[]{:S(2)}) collective-permute-start(bf16[5,3,1,256]{3,1,2,0:T(4,128)(2,1)S(1)} %copy.383), channel_id=1, source_target_pairs={{1,0},{2,1},{3,2},{4,3},{5,4},{6,5},{7,6},{0,7},{9,8},{10,9},{11,1... | collective-permute-start | bytes 23048 | tf_op jit(solution)/shard_map/ppermute | solution.py:21
  35.6 6.1 %collective-permute-start.6 = (bf16[5,3,1,256]{3,1,2,0:T(4,128)(2,1)S(1)}, bf16[5,3,1,256]{3,1,2,0:T(4,128)(2,1)S(1)}, u32[]{:S(2)}, u32[]{:S(2)}) collective-permute-start(bf16[5,3,1,256]{3,1,2,0:T(4,128)(2,1)S(1)} %copy.382), channel_id=1, source_target_pairs={{0,1},{1,2},{2,3},{3,4},{4,5},{5,6},{6,7},{7,0},{8,9},{9,10},{10,1... | collective-permute-start | bytes 23048 | tf_op jit(solution)/shard_map/ppermute | solution.py:18
  42.3 7.0 %collective-permute-start.9 = (bf16[5,1,8,256]{3,2,0,1:T(8,128)(2,1)S(1)}, bf16[5,1,8,256]{3,2,0,1:T(8,128)(2,1)S(1)}, u32[]{:S(2)}, u32[]{:S(2)}) collective-permute-start(bf16[5,1,8,256]{3,2,0,1:T(8,128)(2,1)S(1)} %fusion.78), channel_id=1, source_target_pairs={{8,0},{16,8},{24,16},{32,24},{40,32},{48,40},{56,48},{64,56},{72,6... | collective-permute-start | bytes 61448 | tf_op jit(solution)/shard_map/ppermute | solution.py:21
  48.5 1.2 collective-permute-start.8
  49.7 4.1 %collective-permute-start.11 = (bf16[5,3,1,256]{3,1,2,0:T(4,128)(2,1)S(1)}, bf16[5,3,1,256]{3,1,2,0:T(4,128)(2,1)S(1)}, u32[]{:S(2)}, u32[]{:S(2)}) collective-permute-start(bf16[5,3,1,256]{3,1,2,0:T(4,128)(2,1)S(1)} %copy.395), channel_id=1, source_target_pairs={{1,0},{2,1},{3,2},{4,3},{5,4},{6,5},{7,6},{0,7},{9,8},{10,9},{11,1... | collective-permute-start | bytes 23048 | tf_op jit(solution)/shard_map/ppermute | solution.py:21
  49.8 6.2 %collective-permute-start.10 = (bf16[5,3,1,256]{3,1,2,0:T(4,128)(2,1)S(1)}, bf16[5,3,1,256]{3,1,2,0:T(4,128)(2,1)S(1)}, u32[]{:S(2)}, u32[]{:S(2)}) collective-permute-start(bf16[5,3,1,256]{3,1,2,0:T(4,128)(2,1)S(1)} %copy.394), channel_id=1, source_target_pairs={{0,1},{1,2},{2,3},{3,4},{4,5},{5,6},{6,7},{7,0},{8,9},{9,10},{10,1... | collective-permute-start | bytes 23048 | tf_op jit(solution)/shard_map/ppermute | solution.py:18
  56.4 6.3 %collective-permute-start.13 = (bf16[5,1,8,256]{3,2,0,1:T(8,128)(2,1)S(1)}, bf16[5,1,8,256]{3,2,0,1:T(8,128)(2,1)S(1)}, u32[]{:S(2)}, u32[]{:S(2)}) collective-permute-start(bf16[5,1,8,256]{3,2,0,1:T(8,128)(2,1)S(1)} %get-tuple-element.31), channel_id=1, source_target_pairs={{8,0},{16,8},{24,16},{32,24},{40,32},{48,40},{56,48},{64,56},{72,6... | collective-permute-start | bytes 61448 | tf_op jit(solution)/shard_map/ppermute | solution.py:21
  61.9 1.2 collective-permute-start.12
  63.1 4.1 %collective-permute-start.15 = (bf16[5,3,1,256]{3,1,2,0:T(4,128)(2,1)S(1)}, bf16[5,3,1,256]{3,1,2,0:T(4,128)(2,1)S(1)}, u32[]{:S(2)}, u32[]{:S(2)}) collective-permute-start(bf16[5,3,1,256]{3,1,2,0:T(4,128)(2,1)S(1)} %copy.406), channel_id=1, source_target_pairs={{1,0},{2,1},{3,2},{4,3},{5,4},{6,5},{7,6},{0,7},{9,8},{10,9},{11,1... | collective-permute-start | bytes 23048 | tf_op jit(solution)/shard_map/ppermute | solution.py:21
  63.2 6.2 %collective-permute-start.14 = (bf16[5,3,1,256]{3,1,2,0:T(4,128)(2,1)S(1)}, bf16[5,3,1,256]{3,1,2,0:T(4,128)(2,1)S(1)}, u32[]{:S(2)}, u32[]{:S(2)}) collective-permute-start(bf16[5,3,1,256]{3,1,2,0:T(4,128)(2,1)S(1)} %copy.405), channel_id=1, source_target_pairs={{0,1},{1,2},{2,3},{3,4},{4,5},{5,6},{6,7},{7,0},{8,9},{9,10},{10,1... | collective-permute-start | bytes 23048 | tf_op jit(solution)/shard_map/ppermute | solution.py:18
  73.3 10.3 %all-to-all-start = ((bf16[8,2,2560]{2,1,0:T(2,128)(2,1)}), bf16[8,2,2560]{2,1,0:T(2,128)(2,1)S(1)}, u32[]{:S(2)}, u32[]{:S(2)}) async-start(bf16[8,2,2560]{2,1,0:T(2,128)(2,1)} %reshape.630), calls=%async_computation | async-start | bytes 163840 | tf_op jit(solution)/shard_map/all_to_all | solution.py:90
  76.6 123.3 %all-reduce.3.cloned.1.call-start = ((), (), s32[]{:S(2)}) async-start(), calls=%async_computation.1 | async-start | bytes 131072 | tf_op jit(solution)/shard_map/psum | solution.py:106
  90.1 193.8 %all-reduce.5.cloned.1.call-start = ((), (), s32[]{:S(2)}) async-start(), calls=%async_computation.2 | async-start | bytes 131072 | tf_op jit(solution)/shard_map/psum | solution.py:106
Sparse Core Ops, SparseCore 0:
  90.2 109.6 all-reduce.2
  202.4 81.4 all-reduce.4
